TPU v7x, 32 devices: a whole 2x2x4 slice. The times are simulated.
32 devices in a mesh: lat: 16 (over z, y, x), lev: 2 (over core).
Axes of the slice: x: 2, y: 2, z: 4, core: 2. Of those that a mesh axis runs over, the one named last changes fastest.
Arguments:
- grid: bfloat16 [96, 2, 48, 400], P('lat', None, 'lev'), may hold values from -6 to 6
- point_counts: int32 [96], P('lat'), may hold values from 16 to 400, as said below
- waves: int32 [96], replicated, may hold values from 0 to 95, each once
- legendre: bfloat16 [96, 96, 96], P('lat'), may hold values from -0.625 to 0.625
- weights: float32 [96], P('lat'), may hold values from 0.5 to 2
- stiffness: float32 [48], replicated, may hold values from 1e-06 to 0.0001
Outputs:
- grid_out: bfloat16 [96, 2, 48, 400], P('lat', None, 'lev')
Inputs may be any that keep to these rules, and one draw needn't show every extreme that they name: point_counts[j] is 4 j + 16 or 4 j + 20 (j counted from 0 at the pole), and the last pair has exactly 400 points. `waves`: each wavenumber from 0 to 95 appears once.
All inputs are finite; a program needn't handle non-finite values.
Results may differ from a plain program's by a relative error of at most 0.015.
Values may be sent and summed in bfloat16 or wider, within the bound.
No kernel may reach another device: no remote copies, remote signals or barrier semaphores. Data moves between devices by JAX's collectives and lax.ppermute only.
A program may use at most 128 MiB of HBM per device.

v0:
```python
import math
import jax
import jax.numpy as jnp
from jax import lax
from jax.sharding import PartitionSpec as P

TWO_PI = 2.0 * math.pi
FINE_STEPS = 32


def fourier_tables(count, wavenumbers, quarter_max):
    quarter = count // 4
    step_angle = TWO_PI / quarter.astype(jnp.float32)
    coarse_count = (quarter_max + FINE_STEPS - 1) // FINE_STEPS
    coarse_pos = FINE_STEPS * jnp.arange(coarse_count, dtype=jnp.int32)
    fine_pos = jnp.arange(FINE_STEPS, dtype=jnp.int32)
    coarse_angle = (coarse_pos[:, None] * wavenumbers[None, :] % quarter).astype(
        jnp.float32
    ) * step_angle
    fine_angle = (fine_pos[:, None] * wavenumbers[None, :] % quarter).astype(
        jnp.float32
    ) * step_angle
    coarse_cos = jnp.cos(coarse_angle)[:, None, :]
    coarse_sin = jnp.sin(coarse_angle)[:, None, :]
    fine_cos = jnp.cos(fine_angle)[None, :, :]
    fine_sin = jnp.sin(fine_angle)[None, :, :]
    full_cos = (coarse_cos * fine_cos - coarse_sin * fine_sin).reshape(
        coarse_count * FINE_STEPS, -1
    )[:quarter_max]
    full_sin = (coarse_sin * fine_cos + coarse_cos * fine_sin).reshape(
        coarse_count * FINE_STEPS, -1
    )[:quarter_max]
    positions = jnp.arange(quarter_max, dtype=jnp.int32)
    inside = (positions < quarter)[:, None]
    cosine = jnp.where(inside, full_cos, 0.0)
    sine = jnp.where(inside, full_sin, 0.0)
    matrix = jnp.concatenate([cosine, sine], axis=1).astype(jnp.bfloat16)
    offsets = jnp.arange(4, dtype=jnp.int32)
    twist = offsets[:, None] * wavenumbers[None, :] % count
    theta = twist.astype(jnp.float32) * (TWO_PI / count.astype(jnp.float32))
    return (matrix, jnp.cos(theta), jnp.sin(theta))


def helmholtz(spectra, wavenumbers, offsets, stiffness_local, width):
    full_shape = spectra.shape
    quartered = spectra.reshape(full_shape[:-2] + (full_shape[-2] // 4, 2, 2, full_shape[-1]))
    parity = (1 - 2 * (offsets % 2)).astype(jnp.float32)
    combined = quartered[..., 0, :] + parity * quartered[..., 1, :]
    degrees = (wavenumbers + offsets).astype(jnp.float32)
    inside_band = offsets < width - wavenumbers
    factor = 1.0 / (
        1.0 + stiffness_local[:, None] * degrees[..., None, :] * (degrees[..., None, :] + 1.0)
    )
    damping = jnp.where(inside_band[..., None, :], factor, 0.0)
    scaled = (combined * damping[..., :, None, :]).astype(jnp.bfloat16)
    flipped = scaled * parity.astype(jnp.bfloat16)
    return jnp.stack([scaled, flipped], axis=-2).reshape(full_shape)


def spectral(received, wavenumbers, basis, stiffness_local):
    width = basis.shape[2]
    spectra = jnp.einsum("jcr,cjl->crl", received, basis, preferred_element_type=jnp.float32)
    offsets = jnp.arange(width, dtype=jnp.int32)
    operand = helmholtz(spectra, wavenumbers[:, None], offsets, stiffness_local, width)
    returned = jnp.einsum("crl,cjl->jcr", operand, basis, preferred_element_type=jnp.float32)
    return returned.astype(jnp.bfloat16)


def on_device(grid, point_counts, waves, legendre, weights, stiffness):
    pairs, _, fields, points = grid.shape
    quarter_max = points // 4
    width = waves.shape[0]
    held_slots = legendre.shape[0]
    lat_index = lax.axis_index("lat")
    lev_index = lax.axis_index("lev")

    def analyse(pieces):
        latitude, count, weight = pieces
        matrix, twist_cos, twist_sin = fourier_tables(count, waves, quarter_max)
        values = latitude.reshape(2, fields, quarter_max, 4)
        partial_value = jnp.einsum(
            "hfab,at->hfbt", values, matrix, preferred_element_type=jnp.float32
        )
        cos_part = partial_value[..., :width]
        sin_part = partial_value[..., width:]
        real = jnp.sum(twist_cos * cos_part - twist_sin * sin_part, axis=2)
        imag = -jnp.sum(twist_sin * cos_part + twist_cos * sin_part, axis=2)
        factor = jnp.where(2 * waves < count, weight / count.astype(jnp.float32), 0.0)
        stacked = jnp.stack([real * factor, imag * factor], axis=0)
        packed = jnp.transpose(stacked, (3, 2, 0, 1)).reshape(width, 4 * fields)
        return (packed.astype(jnp.bfloat16), matrix, twist_cos, twist_sin)

    coefficients, matrices, twist_cos, twist_sin = lax.map(analyse, (grid, point_counts, weights))
    received = lax.all_to_all(coefficients, "lat", split_axis=1, concat_axis=0, tiled=True)
    owned = lax.dynamic_slice_in_dim(waves, lat_index * held_slots, held_slots)
    own_stiffness = lax.dynamic_slice_in_dim(stiffness, lev_index * fields, fields)
    synthesised = spectral(received, owned, legendre, own_stiffness)
    returned = lax.all_to_all(synthesised, "lat", split_axis=0, concat_axis=1, tiled=True)

    def synthesise(pieces):
        packed, matrix, turn_cos, turn_sin, count = pieces
        values = packed.astype(jnp.float32).reshape(width, fields, 2, 2)
        real = values[:, :, 0, :]
        imag = values[:, :, 1, :]
        factor = jnp.where(2 * waves < count, jnp.where(waves == 0, 1.0, 2.0), 0.0)[:, None, None]
        cosines = turn_cos[:, :, None, None]
        sines = turn_sin[:, :, None, None]
        turned_real = factor * (real * cosines - imag * sines)
        turned_imag = factor * (real * sines + imag * cosines)
        operand = jnp.concatenate([turned_real, -turned_imag], axis=1)
        upper = operand.astype(jnp.bfloat16)
        lower = (operand - upper.astype(jnp.float32)).astype(jnp.bfloat16)
        result = jnp.einsum("bmfh,am->hfab", upper, matrix, preferred_element_type=jnp.float32)
        result = result + jnp.einsum(
            "bmfh,am->hfab", lower, matrix, preferred_element_type=jnp.float32
        )
        return result.reshape(2, fields, points).astype(jnp.bfloat16)

    return lax.map(synthesise, (returned, matrices, twist_cos, twist_sin, point_counts))


def solution(mesh):
    in_specs = (P("lat", None, "lev", None), P("lat"), P(), P("lat", None, None), P("lat"), P())
    out_specs = P("lat", None, "lev", None)
    return jax.shard_map(
        on_device, mesh=mesh, in_specs=in_specs, out_specs=out_specs, check_vma=False
    )
```

profile of v0, /device:TPU:0, one launch (start us, length us, event | category | flops | bytes accessed | tf_op | source)
XLA Modules:
  0.0 100.6 jit_solution(9834222721202018338)
XLA Ops:
  0.0 0.7 copy-done.1
  0.7 53.4 %while.28 = (s32[]{:T(128)}, bf16[6,96,96]{1,2,0:T(8,128)(2,1)S(1)}, bf16[6,100,192]{1,2,0:T(8,128)(2,1)S(1)}, f32[6,4,96]{2,1,0:T(4,128)S(1)}, f32[6,4,96]{2,1,...) while((s32[]{:T(128)}, ...), condition=%wide.region_3.4_spmd, body=%wide.region_0.3_spmd.sunk | while | flops 7857060 | bytes 1186901 | solution.py:93
  0.7 0.6 dynamic_slice.69
  3.6 0.3 fusion.72
  6.2 0.8 constant_dynamic-slice_fusion.4
  7.5 0.6 dynamic_slice.70
  8.8 0.6 compare_select_fusion.5
  9.6 0.6 dynamic_slice.69
  12.5 0.3 fusion.72
  14.6 0.2 fusion.73
  15.1 0.8 constant_dynamic-slice_fusion.4
  16.5 0.6 dynamic_slice.70
  17.7 0.6 compare_select_fusion.5
  18.5 0.6 dynamic_slice.69
  21.4 0.3 fusion.72
  23.5 0.2 fusion.73
  24.0 0.8 constant_dynamic-slice_fusion.4
  25.4 0.6 dynamic_slice.70
  26.6 0.6 compare_select_fusion.5
  27.4 0.6 dynamic_slice.69
  30.3 0.3 fusion.72
  32.4 0.2 fusion.73
  32.9 0.8 constant_dynamic-slice_fusion.4
  34.3 0.6 dynamic_slice.70
  35.5 0.6 compare_select_fusion.5
  36.3 0.6 dynamic_slice.69
  39.2 0.3 fusion.72
  41.9 0.8 constant_dynamic-slice_fusion.4
  43.2 0.6 dynamic_slice.70
  44.4 0.6 compare_select_fusion.5
  45.2 0.6 dynamic_slice.69
  48.1 0.3 fusion.72
  50.8 0.8 constant_dynamic-slice_fusion.4
  52.1 0.6 dynamic_slice.70
  53.3 0.6 compare_select_fusion.5
  54.1 0.8 copy.35
  55.0 8.4 %all-to-all-start = ((bf16[6,96,96]{2,0,1:T(8,128)(2,1)}), bf16[6,96,96]{2,0,1:T(8,128)(2,1)S(1)}, u32[]{:S(2)}, u32[]{:S(2)}) async-start(bf16[6,96,96]{2,0,1:T(8,128)(2,1)} %copy.35), calls=%async_computation | async-start | bytes 393216 | tf_op jit(solution)/shard_map/all_to_all | solution.py:94
  63.7 0.7 copy-done.4
  64.5 7.5 %all-to-all-done = bf16[6,96,96]{2,0,1:T(8,128)(2,1)S(1)} async-done(((bf16[6,96,96]{2,0,1:T(8,128)(2,1)}), bf16[6,96,96]{2,0,1:T(8,128)(2,1)S(1)}, u32[]{:S(2)}, u32[]{:S(2)}) %all-to-all-start) | async-done | bytes 110624 | tf_op jit(solution)/shard_map/all_to_all | solution.py:94
  72.4 0.3 broadcast_multiply_fusion
  72.7 0.4 pad_maximum_fusion.1
  73.3 0.8 copy.39
  74.1 3.5 %all-to-all-start.1 = ((bf16[96,6,96]{2,1,0:T(8,128)(2,1)}), bf16[96,6,96]{2,1,0:T(8,128)(2,1)S(1)}, u32[]{:S(2)}, u32[]{:S(2)}) async-start(bf16[96,6,96]{2,1,0:T(8,128)(2,1)} %copy.39), calls=%async_computation.1 | async-start | bytes 393216 | tf_op jit(solution)/shard_map/all_to_all | solution.py:98
  77.7 8.0 %all-to-all-done.1 = bf16[96,6,96]{2,1,0:T(8,128)(2,1)S(1)} async-done(((bf16[96,6,96]{2,1,0:T(8,128)(2,1)}), bf16[96,6,96]{2,1,0:T(8,128)(2,1)S(1)}, u32[]{:S(2)}, u32[]{:S(2)}) %all-to-all-start.1) | async-done | bytes 110624 | tf_op jit(solution)/shard_map/all_to_all | solution.py:98
  85.8 14.0 %while.29 = (s32[]{:T(128)}, bf16[6,2,24,400]{3,2,1,0:T(8,128)(2,1)S(1)}, bf16[6,100,192]{1,2,0:T(8,128)(2,1)S(1)}, s32[96]{0:T(128)S(1)}, s32[6]{0:T(128)S(1)},...) while((s32[]{:T(128)}, ...), condition=%wide.region_5.6_spmd, body=%wide.region_4.5_spmd.sunk | while | flops 15291362 | bytes 1428225 | solution.py:119
  86.1 0.6 dynamic_slice.75
  86.7 0.6 compare_select_fusion.6
  87.6 0.2 fusion.80
  88.4 0.6 dynamic_slice.75
  89.0 0.6 compare_select_fusion.6
  89.9 0.2 fusion.80
  90.8 0.6 dynamic_slice.75
  91.4 0.6 compare_select_fusion.6
  92.3 0.2 fusion.80
  93.1 0.6 dynamic_slice.75
  93.7 0.6 compare_select_fusion.6
  94.6 0.2 fusion.80
  95.4 0.6 dynamic_slice.75
  96.0 0.6 compare_select_fusion.6
  97.0 0.2 fusion.80
  97.8 0.6 dynamic_slice.75
  98.4 0.6 compare_select_fusion.6
  99.3 0.2 fusion.80
  99.9 0.7 copy-done.2
  (204 shorter events, 12.7 us)
Async XLA Ops:
  0.0 72.1 %copy-start = (bf16[6,96,96]{2,1,0:T(8,128)(2,1)S(1)}, bf16[6,96,96]{2,1,0:T(8,128)(2,1)}, u32[]{:S(2)}) copy-start(bf16[6,96,96]{2,1,0:T(8,128)(2,1)} %param.13) | copy-start | bytes 331780
  0.0 0.7 copy-start.1
  0.0 0.7 copy-start.3
  0.0 0.7 copy-start.5
  55.0 17.0 %all-to-all-start = ((bf16[6,96,96]{2,0,1:T(8,128)(2,1)}), bf16[6,96,96]{2,0,1:T(8,128)(2,1)S(1)}, u32[]{:S(2)}, u32[]{:S(2)}) async-start(bf16[6,96,96]{2,0,1:T(8,128)(2,1)} %copy.35), calls=%async_computation | async-start | bytes 393216 | tf_op jit(solution)/shard_map/all_to_all | solution.py:94
  63.7 0.7 copy-start.4
  74.1 11.6 %all-to-all-start.1 = ((bf16[96,6,96]{2,1,0:T(8,128)(2,1)}), bf16[96,6,96]{2,1,0:T(8,128)(2,1)S(1)}, u32[]{:S(2)}, u32[]{:S(2)}) async-start(bf16[96,6,96]{2,1,0:T(8,128)(2,1)} %copy.39), calls=%async_computation.1 | async-start | bytes 393216 | tf_op jit(solution)/shard_map/all_to_all | solution.py:98
  99.9 0.7 copy-start.2
where the time goes:
time: 102 us; the launch traced here: 101 us
  loops' own time  29.3 us (29%)
  local copies, waits for them, and re-layouts  24.9 us (24%)
  waiting for transfers between devices  15.5 us (15%)
  other arithmetic  14.2 us (14%)
  starting transfers between devices  11.9 us (12%)
  matrix products  4.6 us (5%)
    another operation x1, loops' own time, on_device(): lax.map(analyse, (grid, point_counts, weights))  28.8 us
    dynamic_slice x30, local copies, waits for them, and re-layouts, on_device(): lax.map(analyse, (grid, point_counts, weights))  16.5 us
    all_to_all x1, starting transfers between devices, on_device(): lax.all_to_all(coefficients, 'lat', split_axis=1, concat_axis=0, tiled=True)  8.35 us
    all_to_all x1, waiting for transfers between devices, on_device(): lax.all_to_all(synthesised, 'lat', split_axis=0, concat_axis=1, tiled=True)  8.03 us
    all_to_all x1, waiting for transfers between devices, on_device(): lax.all_to_all(coefficients, 'lat', split_axis=1, concat_axis=0, tiled=True)  7.5 us
    select_n x6, other arithmetic, synthesise(): jnp.where(2 * waves < count, jnp.where(waves == 0, 1.0, 2.0), 0.0)  3.89 us
    all_to_all x1, starting transfers between devices, on_device(): lax.all_to_all(synthesised, 'lat', split_axis=0, concat_axis=1, tiled=True)  3.52 us
    select_n x6, other arithmetic, analyse(): jnp.where(2 * waves < count, weight / count.astype(jnp.float32), 0.0)  3.37 us
  transfers between devices with their start and end apart: 2, of which 2 were waited for; matrix products, arithmetic and copies ran while one was open for 0% of the time, Pallas kernels for 0%

commit v1 on v0

--- a/solution.py
+++ b/solution.py
@@ -1,11 +1,23 @@
+import functools
 import math
 import jax
 import jax.numpy as jnp
 from jax import lax
 from jax.sharding import PartitionSpec as P
+from jax.lax import all_to_all, axis_size
 
 TWO_PI = 2.0 * math.pi
 FINE_STEPS = 32
+
+
+def plan_tails(v0, peer_axis):
+    return jnp.concatenate(
+        all_to_all(jnp.stack(jnp.split(v0, axis_size(peer_axis), axis=0), axis=0), peer_axis, 0, 0),
+        1,
+    )
+
+
+press_rails = functools.partial(plan_tails, peer_axis="lat")
 
 
 def fourier_tables(count, wavenumbers, quarter_max):
@@ -95,7 +107,7 @@
     owned = lax.dynamic_slice_in_dim(waves, lat_index * held_slots, held_slots)
     own_stiffness = lax.dynamic_slice_in_dim(stiffness, lev_index * fields, fields)
     synthesised = spectral(received, owned, legendre, own_stiffness)
-    returned = lax.all_to_all(synthesised, "lat", split_axis=0, concat_axis=1, tiled=True)
+    returned = press_rails(synthesised)
 
     def synthesise(pieces):
         packed, matrix, turn_cos, turn_sin, count = pieces

time: 102 us -> 110 us (1.078)
  local copies, waits for them, and re-layouts: 24.9 us -> 33.2 us
    unnamed x12 -> x27, local copies, waits for them, and re-layouts: 2.07 us -> 11.1 us
where the time goes in v1:
time: 110 us; the launch traced here: 109 us
  local copies, waits for them, and re-layouts  33.2 us (30%)
  loops' own time  29.3 us (27%)
  waiting for transfers between devices  15.5 us (14%)
  other arithmetic  14.2 us (13%)
  starting transfers between devices  11.9 us (11%)
  matrix products  4.6 us (4%)
    another operation x1, loops' own time, on_device(): lax.map(analyse, (grid, point_counts, weights))  28.8 us
    dynamic_slice x30, local copies, waits for them, and re-layouts, on_device(): lax.map(analyse, (grid, point_counts, weights))  16.5 us
    unnamed x27, local copies, waits for them, and re-layouts  11.1 us
    all_to_all x1, starting transfers between devices, on_device(): lax.all_to_all(coefficients, 'lat', split_axis=1, concat_axis=0, tiled=True)  8.35 us
    all_to_all x1, waiting for transfers between devices, plan_tails(): all_to_all(jnp.stack(jnp.split(v0, axis_size(peer_axis), axis=0), axis=0)...  8.03 us
    all_to_all x1, waiting for transfers between devices, on_device(): lax.all_to_all(coefficients, 'lat', split_axis=1, concat_axis=0, tiled=True)  7.5 us
    select_n x6, other arithmetic, synthesise(): jnp.where(2 * waves < count, jnp.where(waves == 0, 1.0, 2.0), 0.0)  3.89 us
    all_to_all x1, starting transfers between devices, plan_tails(): all_to_all(jnp.stack(jnp.split(v0, axis_size(peer_axis), axis=0), axis=0)...  3.52 us
  transfers between devices with their start and end apart: 2, of which 2 were waited for; matrix products, arithmetic and copies ran while one was open for 0% of the time, Pallas kernels for 0%

profile of v1, /device:TPU:0, one launch (start us, length us, event | category | flops | bytes accessed | tf_op | source)
XLA Modules:
  0.0 108.8 jit_solution(6132496719779512285)
XLA Ops:
  0.0 0.7 copy-done.1
  0.7 53.4 %while.28 = (s32[]{:T(128)}, bf16[6,96,96]{1,2,0:T(8,128)(2,1)S(1)}, bf16[6,100,192]{1,2,0:T(8,128)(2,1)S(1)}, f32[6,4,96]{2,1,0:T(4,128)S(1)}, f32[6,4,96]{2,1,...) while((s32[]{:T(128)}, ...), condition=%wide.region_3.4_spmd, body=%wide.region_0.3_spmd.sunk | while | flops 7857060 | bytes 1186901 | solution.py:105
  0.7 0.6 dynamic_slice.69
  6.2 0.8 constant_dynamic-slice_fusion.4
  7.5 0.6 dynamic_slice.70
  8.8 0.6 compare_select_fusion.5
  9.6 0.6 dynamic_slice.69
  15.1 0.8 constant_dynamic-slice_fusion.4
  16.5 0.6 dynamic_slice.70
  17.7 0.6 compare_select_fusion.5
  18.5 0.6 dynamic_slice.69
  24.0 0.8 constant_dynamic-slice_fusion.4
  25.4 0.6 dynamic_slice.70
  26.6 0.6 compare_select_fusion.5
  27.4 0.6 dynamic_slice.69
  33.0 0.8 constant_dynamic-slice_fusion.4
  34.3 0.6 dynamic_slice.70
  35.5 0.6 compare_select_fusion.5
  36.3 0.6 dynamic_slice.69
  41.9 0.8 constant_dynamic-slice_fusion.4
  43.2 0.6 dynamic_slice.70
  44.4 0.6 compare_select_fusion.5
  45.3 0.6 dynamic_slice.69
  50.8 0.8 constant_dynamic-slice_fusion.4
  52.1 0.6 dynamic_slice.70
  53.3 0.6 compare_select_fusion.5
  54.1 0.8 copy.33
  55.0 8.4 %all-to-all-start = ((bf16[6,96,96]{2,0,1:T(8,128)(2,1)}), bf16[6,96,96]{2,0,1:T(8,128)(2,1)S(1)}, u32[]{:S(2)}, u32[]{:S(2)}) async-start(bf16[6,96,96]{2,0,1:T(8,128)(2,1)} %copy.33), calls=%async_computation | async-start | bytes 393216 | tf_op jit(solution)/shard_map/all_to_all | solution.py:106
  63.7 0.7 copy-done.4
  64.5 7.5 %all-to-all-done = bf16[6,96,96]{2,0,1:T(8,128)(2,1)S(1)} async-done(((bf16[6,96,96]{2,0,1:T(8,128)(2,1)}), bf16[6,96,96]{2,0,1:T(8,128)(2,1)S(1)}, u32[]{:S(2)}, u32[]{:S(2)}) %all-to-all-start) | async-done | bytes 110624 | tf_op jit(solution)/shard_map/all_to_all | solution.py:106
  72.4 0.3 broadcast_multiply_fusion
  72.7 0.4 pad_maximum_fusion.1
  73.3 0.6 constant_dynamic-update-slice_fusion.17
  73.9 0.6 constant_dynamic-update-slice_fusion.16
  74.5 0.6 constant_dynamic-update-slice_fusion.15
  75.1 0.6 constant_dynamic-update-slice_fusion.14
  75.7 0.6 constant_dynamic-update-slice_fusion.13
  76.3 0.6 constant_dynamic-update-slice_fusion.12
  76.9 0.6 constant_dynamic-update-slice_fusion.11
  77.5 0.6 constant_dynamic-update-slice_fusion.10
  78.1 0.6 constant_dynamic-update-slice_fusion.9
  78.7 0.6 constant_dynamic-update-slice_fusion.8
  79.4 0.6 constant_dynamic-update-slice_fusion.7
  80.0 0.6 constant_dynamic-update-slice_fusion.6
  80.6 0.6 constant_dynamic-update-slice_fusion.5
  81.2 0.6 constant_dynamic-update-slice_fusion.4
  81.8 0.6 constant_dynamic-update-slice_fusion.3
  82.4 0.6 constant_dynamic-update-slice_fusion.2
  83.0 3.5 %all-to-all-start.1 = ((bf16[16,6,6,96]{3,1,2,0:T(8,128)(2,1)}), bf16[16,6,6,96]{3,1,2,0:T(8,128)(2,1)S(1)}, u32[]{:S(2)}, u32[]{:S(2)}) async-start(bf16[16,6,6,96]{3,1,2,0:T(8,128)(2,1)} %constant_dynamic-update-slice_fusion.2), calls=%async_computation.1 | async-start | bytes 393216 | tf_op jit(solution)/shard_map/all_to_all | solution.py:15
  86.5 8.0 %all-to-all-done.1 = bf16[16,6,6,96]{3,1,2,0:T(8,128)(2,1)S(1)} async-done(((bf16[16,6,6,96]{3,1,2,0:T(8,128)(2,1)}), bf16[16,6,6,96]{3,1,2,0:T(8,128)(2,1)S(1)}, u32[]{:S(2)}, u32[]{:S(2)}) %all-to-all-start.1) | async-done | bytes 110624 | tf_op jit(solution)/shard_map/all_to_all | solution.py:15
  94.7 13.4 %while.29 = (s32[]{:T(128)}, bf16[6,2,24,400]{3,2,1,0:T(8,128)(2,1)S(1)}, bf16[6,100,192]{1,2,0:T(8,128)(2,1)S(1)}, s32[96]{0:T(128)S(1)}, s32[6]{0:T(128)S(1)},...) while((s32[]{:T(128)}, ...), condition=%wide.region_5.6_spmd, body=%wide.region_4.5_spmd.sunk | while | flops 15291362 | bytes 1391361 | solution.py:131
  94.9 0.6 dynamic_slice.75
  95.5 0.6 compare_select_fusion.6
  97.1 0.6 dynamic_slice.75
  97.7 0.6 compare_select_fusion.6
  99.3 0.6 dynamic_slice.75
  99.9 0.6 compare_select_fusion.6
  101.6 0.6 dynamic_slice.75
  102.1 0.6 compare_select_fusion.6
  103.8 0.6 dynamic_slice.75
  104.4 0.6 compare_select_fusion.6
  106.0 0.6 dynamic_slice.75
  106.6 0.6 compare_select_fusion.6
  108.1 0.7 copy-done.2
  (212 shorter events, 16.0 us)
Async XLA Ops:
  0.0 72.1 %copy-start = (bf16[6,96,96]{2,1,0:T(8,128)(2,1)S(1)}, bf16[6,96,96]{2,1,0:T(8,128)(2,1)}, u32[]{:S(2)}) copy-start(bf16[6,96,96]{2,1,0:T(8,128)(2,1)} %param.13) | copy-start | bytes 331780
  0.0 0.7 copy-start.1
  0.0 0.7 copy-start.3
  0.0 0.7 copy-start.5
  55.0 17.0 %all-to-all-start = ((bf16[6,96,96]{2,0,1:T(8,128)(2,1)}), bf16[6,96,96]{2,0,1:T(8,128)(2,1)S(1)}, u32[]{:S(2)}, u32[]{:S(2)}) async-start(bf16[6,96,96]{2,0,1:T(8,128)(2,1)} %copy.33), calls=%async_computation | async-start | bytes 393216 | tf_op jit(solution)/shard_map/all_to_all | solution.py:106
  63.7 0.7 copy-start.4
  83.0 11.6 %all-to-all-start.1 = ((bf16[16,6,6,96]{3,1,2,0:T(8,128)(2,1)}), bf16[16,6,6,96]{3,1,2,0:T(8,128)(2,1)S(1)}, u32[]{:S(2)}, u32[]{:S(2)}) async-start(bf16[16,6,6,96]{3,1,2,0:T(8,128)(2,1)} %constant_dynamic-update-slice_fusion.2), calls=%async_computation.1 | async-start | bytes 393216 | tf_op jit(solution)/shard_map/all_to_all | solution.py:15
  108.1 0.7 copy-start.2
